TPU v7x, 32 devices: a whole 2x2x4 slice. The times are simulated.
32 devices in a mesh: batch: 8 (over y, x, core), tensor: 4 (over z).
Axes of the slice: x: 2, y: 2, z: 4, core: 2. Of those that a mesh axis runs over, the one named last changes fastest.
Arguments:
- slot_states: bfloat16 [960, 32, 768], P('tensor', 'batch'), may hold values from -6 to 6
- pass_counts: int32 [32], P('batch'), may hold values from 2 to 5
- w_qkv: bfloat16 [768, 3, 768], P(None, None, 'tensor'), may hold values from -0.21875 to 0.21875
- q_bias: bfloat16 [768], P('tensor'), may hold values from -3 to 3
- v_bias: bfloat16 [768], P('tensor'), may hold values from -0.29882812 to 0.29882812
- w_out: bfloat16 [768, 768], P('tensor'), may hold values from -1.75 to 1.75
- out_bias: bfloat16 [768], replicated, may hold values from -3 to 3
- w_up: bfloat16 [768, 3072], P(None, 'tensor'), may hold values from -0.21875 to 0.21875
- up_bias: bfloat16 [3072], P('tensor'), may hold values from -3 to 3
- w_down: bfloat16 [3072, 768], P('tensor'), may hold values from -0.109375 to 0.109375
- down_bias: bfloat16 [768], replicated, may hold values from -3 to 3
- ln1_gain: bfloat16 [768], replicated, may hold values from 0.099609375 to 1.8984375
- ln1_bias: bfloat16 [768], replicated, may hold values from -2 to 2
- ln2_gain: bfloat16 [768], replicated, may hold values from 0.099609375 to 1.8984375
- ln2_bias: bfloat16 [768], replicated, may hold values from -2 to 2
- pass_table: bfloat16 [5, 768], replicated, may hold values from -5 to 5
- cotangent: bfloat16 [960, 32, 768], P('tensor', 'batch'), may hold values from -6 to 6
Outputs:
- layer_out: bfloat16 [960, 32, 768], P('tensor', 'batch')
- grad_states: bfloat16 [960, 32, 768], P('tensor', 'batch')
- grad_qkv: float32 [768, 3, 768], P(None, None, 'tensor')
- grad_q_bias: float32 [768], P('tensor')
- grad_v_bias: float32 [768], P('tensor')
- grad_out: float32 [768, 768], P('tensor')
- grad_out_bias: float32 [768], replicated
- grad_up: float32 [768, 3072], P(None, 'tensor')
- grad_up_bias: float32 [3072], P('tensor')
- grad_down: float32 [3072, 768], P('tensor')
- grad_down_bias: float32 [768], replicated
- grad_ln1_gain: float32 [768], replicated
- grad_ln1_bias: float32 [768], replicated
- grad_ln2_gain: float32 [768], replicated
- grad_ln2_bias: float32 [768], replicated
- grad_pass: float32 [5, 768], replicated
All inputs are finite; a program needn't handle non-finite values.
Results may differ from a plain program's by a relative error of at most 0.02.
Values may be sent and summed in bfloat16 or wider, within the bound.
No kernel may reach another device: no remote copies, remote signals or barrier semaphores. Data moves between devices by JAX's collectives and lax.ppermute only.
A program may use at most 256 MiB of HBM per device.

v0:
```python
import math
import jax
import jax.numpy as jnp
from jax import lax
from jax.sharding import PartitionSpec as P

HEAD_DIM = 64
PASSES = 5
LEN = 192
MICRO = 4
SEQ_DEV = 1
HIGHEST = lax.Precision.HIGHEST
EPSILON = 1e-05
MASKED = -1e30


def norm_rows(values, gain, shift):
    center = values - jnp.mean(values, axis=-1, keepdims=True)
    spread = jnp.mean(center * center, axis=-1, keepdims=True)
    return center * lax.rsqrt(spread + EPSILON) * gain + shift


def gelu_tanh(values):
    return jax.nn.gelu(values, approximate=True)


def block_scores(query, keys, allowed, scale):
    scores = jnp.einsum("qbhd,kbhd->bhqk", query, keys, preferred_element_type=jnp.float32) * scale
    return jnp.where(allowed, scores, MASKED)


def attend_block(query, keys, values, allowed, scale):
    scores = block_scores(query, keys, allowed, scale)
    peak = jnp.max(scores, axis=-1, keepdims=True)
    powers = jnp.exp(scores - peak)
    total = jnp.sum(powers, axis=-1, keepdims=True)
    weights = (powers / total).astype(jnp.bfloat16)
    mixed = jnp.einsum("bhqk,kbhd->qbhd", weights, values, preferred_element_type=jnp.float32)
    return (mixed.astype(jnp.bfloat16), peak + jnp.log(total))


def attend_back(query, keys, values, allowed, log_total, grad_mixed, scale):
    scores = block_scores(query, keys, allowed, scale)
    probs = jnp.exp(scores - log_total)
    grad_weights = jnp.einsum(
        "qbhd,kbhd->bhqk", grad_mixed, values, preferred_element_type=jnp.float32
    )
    inner = jnp.sum(probs * grad_weights, axis=-1, keepdims=True)
    grad_scores = (probs * (grad_weights - inner)).astype(jnp.bfloat16)
    grad_query = (
        jnp.einsum("bhqk,kbhd->qbhd", grad_scores, keys, preferred_element_type=jnp.float32) * scale
    )
    grad_keys = (
        jnp.einsum("bhqk,qbhd->kbhd", grad_scores, query, preferred_element_type=jnp.float32)
        * scale
    )
    grad_values = jnp.einsum(
        "bhqk,qbhd->kbhd",
        probs.astype(jnp.bfloat16),
        grad_mixed,
        preferred_element_type=jnp.float32,
    )
    return (grad_query, grad_keys, grad_values)


def layer_block(states, counts, cot_rows, row_index, slots, weights, norms, links):
    qkv_matrix, q_bias, v_bias, w_out, bias_output, w_up, bias_upward, w_down, bias_downward = (
        weights
    )
    gain_one, shift_one, gain_two, shift_two, table = norms
    (
        gather_first,
        sum_attn,
        gather_second,
        sum_mlp,
        gather_grad,
        sum_upward,
        gather_attn,
        sum_qkv,
    ) = links
    width = states.shape[2]
    nseq = states.shape[1]
    local_width = qkv_matrix.shape[1] // 3
    heads_here = local_width // HEAD_DIM
    scale = 1.0 / math.sqrt(HEAD_DIM)
    full_index = jnp.arange(slots, dtype=jnp.int32)
    bias_query = q_bias.astype(jnp.float32).reshape(heads_here, HEAD_DIM)
    bias_value = v_bias.astype(jnp.float32).reshape(heads_here, HEAD_DIM)
    passes = row_index[:, None] % counts[None, :]
    onehot = (passes[:, :, None] == jnp.arange(PASSES, dtype=jnp.int32)[None, None, :]).astype(
        jnp.float32
    )
    live_rows = row_index[:, None] < counts[None, :] * LEN
    allowed = (full_index[None, None, :] <= full_index[None, :, None]) & (
        full_index[None, None, :] < (counts * LEN)[:, None, None]
    )
    hidden = states + jnp.einsum("rbp,pd->rbd", onehot, table, precision=HIGHEST)
    norm_one, pull_one = jax.vjp(norm_rows, hidden, gain_one, shift_one)
    gathered_one = gather_first(norm_one.astype(jnp.bfloat16))
    projected = jnp.einsum(
        "sbd,dc->sbc", gathered_one, qkv_matrix, preferred_element_type=jnp.float32
    )
    projected = projected.reshape(slots, nseq, 3, heads_here, HEAD_DIM)
    query = (projected[:, :, 0] + bias_query).astype(jnp.bfloat16)
    keys = projected[:, :, 1].astype(jnp.bfloat16)
    values = (projected[:, :, 2] + bias_value).astype(jnp.bfloat16)
    piece_number = 0
    begin = piece_number * slots
    mixed, log_total = attend_block(
        query, keys, values, allowed[:, None, begin : begin + slots], scale
    )
    log_blocks = [log_total]
    mixed_flat = mixed.reshape(slots, nseq, local_width)

    def attn_term(start, count):
        return jnp.einsum("sbc,cd->sbd", mixed_flat, w_out, preferred_element_type=jnp.float32)

    attn_total = sum_attn(attn_term)
    after = hidden + attn_total + bias_output
    norm_two, pull_two = jax.vjp(norm_rows, after, gain_two, shift_two)
    gathered_two = gather_second(norm_two.astype(jnp.bfloat16))
    pre_act = (
        jnp.einsum("sbd,df->sbf", gathered_two, w_up, preferred_element_type=jnp.float32)
        + bias_upward
    )
    activated, pull_act = jax.vjp(gelu_tanh, pre_act)
    act_low = activated.astype(jnp.bfloat16)

    def mlp_term(start, count):
        return jnp.einsum("sbf,fd->sbd", act_low, w_down, preferred_element_type=jnp.float32)

    mlp_total = sum_mlp(mlp_term)
    result = after + mlp_total + bias_downward
    layer_part = jnp.where(live_rows[:, :, None], result, 0.0).astype(jnp.bfloat16)
    grad_result = jnp.where(live_rows[:, :, None], cot_rows.astype(jnp.float32), 0.0)
    grad_branch = gather_grad(grad_result.astype(jnp.bfloat16))
    grad_down_part = jnp.einsum(
        "sbf,sbd->fd", act_low, grad_branch, preferred_element_type=jnp.float32
    )
    grad_act = jnp.einsum("sbd,fd->sbf", grad_branch, w_down, preferred_element_type=jnp.float32)
    grad_pre = pull_act(grad_act)[0].astype(jnp.bfloat16)
    grad_up_part = jnp.einsum(
        "sbd,sbf->df", gathered_two, grad_pre, preferred_element_type=jnp.float32
    )
    grad_up_bias_part = jnp.sum(grad_pre.astype(jnp.float32), axis=(0, 1))

    def upward_term(start, count):
        return jnp.einsum("sbf,df->sbd", grad_pre, w_up, preferred_element_type=jnp.float32)

    grad_norm_two = sum_upward(upward_term)
    grad_after, grad_gain_two, grad_shift_two = pull_two(grad_norm_two)
    grad_after = grad_after + grad_result
    grad_out_bias_part = jnp.sum(grad_after, axis=(0, 1))
    grad_down_bias_part = jnp.sum(grad_result, axis=(0, 1))
    grad_attn = gather_attn(grad_after.astype(jnp.bfloat16))
    grad_out_part = jnp.einsum(
        "sbc,sbd->cd", mixed_flat, grad_attn, preferred_element_type=jnp.float32
    )
    grad_mixed = jnp.einsum("sbd,cd->sbc", grad_attn, w_out, preferred_element_type=jnp.float32)
    grad_mixed = grad_mixed.astype(jnp.bfloat16).reshape(slots, nseq, heads_here, HEAD_DIM)
    piece_number = 0
    begin = piece_number * slots
    grad_query, grad_keys, grad_values = attend_back(
        query,
        keys,
        values,
        allowed[:, None, begin : begin + slots],
        log_blocks[piece_number],
        grad_mixed,
        scale,
    )
    grad_proj = jnp.stack([grad_query, grad_keys, grad_values], axis=2)
    grad_proj = grad_proj.astype(jnp.bfloat16).reshape(slots, nseq, 3 * local_width)
    grad_qkv_part = jnp.einsum(
        "sbd,sbc->dc", gathered_one, grad_proj, preferred_element_type=jnp.float32
    ).reshape(width, 3, local_width)
    rounded_proj = grad_proj.astype(jnp.float32).reshape(slots, nseq, 3, local_width)
    grad_q_bias_part = jnp.sum(rounded_proj[:, :, 0], axis=(0, 1))
    grad_v_bias_part = jnp.sum(rounded_proj[:, :, 2], axis=(0, 1))

    def qkv_term(start, count):
        return jnp.einsum("sbc,dc->sbd", grad_proj, qkv_matrix, preferred_element_type=jnp.float32)

    grad_norm_one = sum_qkv(qkv_term)
    grad_hidden, grad_gain_one, grad_shift_one = pull_one(grad_norm_one)
    grad_hidden = grad_hidden + grad_after
    grad_part = grad_hidden.astype(jnp.bfloat16)
    grad_pass_part = jnp.einsum("rbp,rbd->pd", onehot, grad_hidden, precision=HIGHEST)
    matrices = (grad_qkv_part, grad_out_part, grad_up_part, grad_down_part)
    shared = (
        grad_gain_one,
        grad_shift_one,
        grad_gain_two,
        grad_shift_two,
        grad_out_bias_part,
        grad_down_bias_part,
        grad_pass_part,
    )
    biases = (grad_q_bias_part, grad_v_bias_part, grad_up_bias_part)
    return (layer_part, grad_part, matrices, shared, biases)


def add_tuples(old, new):
    if old is None:
        return new
    return tuple((first + second for first, second in zip(old, new)))


def per_device(
    slot_states,
    pass_counts,
    w_qkv,
    q_bias,
    v_bias,
    w_out,
    out_bias,
    w_up,
    up_bias,
    w_down,
    down_bias,
    ln1_gain,
    ln1_bias,
    ln2_gain,
    ln2_bias,
    pass_table,
    cotangent,
):
    groups = lax.axis_size("tensor")
    rows = slot_states.shape[0]
    slots = rows * groups
    norms = (
        ln1_gain.astype(jnp.float32),
        ln1_bias.astype(jnp.float32),
        ln2_gain.astype(jnp.float32),
        ln2_bias.astype(jnp.float32),
        pass_table.astype(jnp.float32),
    )
    bias_output = out_bias.astype(jnp.float32)
    bias_downward = down_bias.astype(jnp.float32)
    layer_parts = []
    grad_parts = []
    matrix_totals = None
    shared_totals = None
    bias_totals = None
    width = slot_states.shape[2]
    weights = (
        w_qkv.reshape(width, 3 * w_qkv.shape[2]),
        q_bias,
        v_bias,
        w_out,
        bias_output,
        w_up,
        up_bias.astype(jnp.float32),
        w_down,
        bias_downward,
    )
    row_index = lax.axis_index("tensor") * rows + jnp.arange(rows, dtype=jnp.int32)

    def gather_first(values):
        return lax.all_gather(values, "tensor", axis=0, tiled=True)

    def sum_attn(term):
        return lax.psum_scatter(
            term(jnp.int32(0), lax.axis_size("tensor") * rows).astype(jnp.bfloat16),
            "tensor",
            scatter_dimension=0,
            tiled=True,
        ).astype(jnp.float32)

    def gather_second(values):
        return lax.all_gather(values, "tensor", axis=0, tiled=True)

    def sum_mlp(term):
        return lax.psum_scatter(
            term(jnp.int32(0), lax.axis_size("tensor") * rows).astype(jnp.bfloat16),
            "tensor",
            scatter_dimension=0,
            tiled=True,
        ).astype(jnp.float32)

    def gather_grad(values):
        return lax.all_gather(values, "tensor", axis=0, tiled=True)

    def sum_upward(term):
        return lax.psum_scatter(
            term(jnp.int32(0), lax.axis_size("tensor") * rows).astype(jnp.bfloat16),
            "tensor",
            scatter_dimension=0,
            tiled=True,
        ).astype(jnp.float32)

    def gather_attn(values):
        return lax.all_gather(values, "tensor", axis=0, tiled=True)

    def sum_qkv(term):
        return lax.psum_scatter(
            term(jnp.int32(0), lax.axis_size("tensor") * rows).astype(jnp.bfloat16),
            "tensor",
            scatter_dimension=0,
            tiled=True,
        ).astype(jnp.float32)

    links = (
        gather_first,
        sum_attn,
        gather_second,
        sum_mlp,
        gather_grad,
        sum_upward,
        gather_attn,
        sum_qkv,
    )
    for micro in range(MICRO):
        first_seq = micro * SEQ_DEV
        layer_part, grad_part, matrices, shared, biases = layer_block(
            slot_states[:, first_seq : first_seq + SEQ_DEV].astype(jnp.float32),
            pass_counts[first_seq : first_seq + SEQ_DEV],
            cotangent[:, first_seq : first_seq + SEQ_DEV],
            row_index,
            slots,
            weights,
            norms,
            links,
        )
        layer_parts.append(layer_part)
        grad_parts.append(grad_part)
        matrices = (
            lax.psum_scatter(matrices[0], "batch", scatter_dimension=0, tiled=True),
            lax.psum_scatter(matrices[1], "batch", scatter_dimension=0, tiled=True),
            lax.psum_scatter(matrices[2], "batch", scatter_dimension=0, tiled=True),
            lax.psum_scatter(matrices[3], "batch", scatter_dimension=0, tiled=True),
        )
        matrix_totals = add_tuples(matrix_totals, matrices)
        shared_totals = add_tuples(shared_totals, shared)
        bias_totals = add_tuples(bias_totals, biases)
    layer_out = jnp.concatenate(layer_parts, axis=1)
    grad_states = jnp.concatenate(grad_parts, axis=1)
    whole = (
        lax.all_gather(matrix_totals[0].astype(jnp.bfloat16), "batch", axis=0, tiled=True).astype(
            jnp.float32
        ),
        lax.all_gather(matrix_totals[1].astype(jnp.bfloat16), "batch", axis=0, tiled=True).astype(
            jnp.float32
        ),
        lax.all_gather(matrix_totals[2].astype(jnp.bfloat16), "batch", axis=0, tiled=True).astype(
            jnp.float32
        ),
        lax.all_gather(matrix_totals[3].astype(jnp.bfloat16), "batch", axis=0, tiled=True).astype(
            jnp.float32
        ),
    )
    shared_sum = lax.psum(
        (
            shared_totals[0],
            shared_totals[1],
            shared_totals[2],
            shared_totals[3],
            shared_totals[4],
            shared_totals[5],
            shared_totals[6],
        ),
        ("batch", "tensor"),
    )
    bias_sum = lax.psum((bias_totals[0], bias_totals[1], bias_totals[2]), "batch")
    return (
        layer_out,
        grad_states,
        whole[0],
        bias_sum[0],
        bias_sum[1],
        whole[1],
        shared_sum[4],
        whole[2],
        bias_sum[2],
        whole[3],
        shared_sum[5],
        shared_sum[0],
        shared_sum[1],
        shared_sum[2],
        shared_sum[3],
        shared_sum[6],
    )


def solution(mesh):
    in_specs = (
        P("tensor", "batch", None),
        P("batch"),
        P(None, None, "tensor"),
        P("tensor"),
        P("tensor"),
        P("tensor", None),
        P(),
        P(None, "tensor"),
        P("tensor"),
        P("tensor", None),
        P(),
        P(),
        P(),
        P(),
        P(),
        P(),
        P("tensor", "batch", None),
    )
    out_specs = (
        P("tensor", "batch", None),
        P("tensor", "batch", None),
        P(None, None, "tensor"),
        P("tensor"),
        P("tensor"),
        P("tensor", None),
        P(),
        P(None, "tensor"),
        P("tensor"),
        P("tensor", None),
        P(),
        P(),
        P(),
        P(),
        P(),
        P(),
    )
    return jax.shard_map(
        per_device, mesh=mesh, in_specs=in_specs, out_specs=out_specs, check_vma=False
    )
```

profile of v0, /device:TPU:0, one launch (start us, length us, event | category | flops | bytes accessed | tf_op | source)
XLA Modules:
  0.0 1458.3 jit_solution(311594064871290279)
XLA Ops:
  15.2 6.8 fusion.308
  37.2 29.7 %all-gather.19.cloned.1.call-done = bf16[960,1,768]{2,0,1:T(8,128)(2,1)} async-done(((bf16[240,1,768]{2,0,1:T(8,128)(2,1)}), bf16[960,1,768]{2,0,1:T(8,128)(2,1)}) %all-gather.19.cloned.1.call-update) | async-done | bytes 1474576 | tf_op jit(solution)/shard_map/all_gather | solution.py:260
  82.1 21.3 %all-gather.23.cloned.1.call-done = bf16[960,1,768]{2,0,1:T(8,128)(2,1)} async-done(((bf16[240,1,768]{2,0,1:T(8,128)(2,1)}), bf16[960,1,768]{2,0,1:T(8,128)(2,1)}) %all-gather.23.cloned.1.call-update) | async-done | bytes 1474576 | tf_op jit(solution)/shard_map/all_gather | solution.py:260
  118.2 21.6 %all-gather.27.cloned.1.call-done = bf16[960,1,768]{2,0,1:T(8,128)(2,1)} async-done(((bf16[240,1,768]{2,0,1:T(8,128)(2,1)}), bf16[960,1,768]{2,0,1:T(8,128)(2,1)}) %all-gather.27.cloned.1.call-update) | async-done | bytes 1474576 | tf_op jit(solution)/shard_map/all_gather | solution.py:260
  154.5 21.2 %all-gather.31.cloned.1.call-done = bf16[960,1,768]{2,0,1:T(8,128)(2,1)} async-done(((bf16[240,1,768]{2,0,1:T(8,128)(2,1)}), bf16[960,1,768]{2,0,1:T(8,128)(2,1)}) %all-gather.31.cloned.1.call-update) | async-done | bytes 1474576 | tf_op jit(solution)/shard_map/all_gather | solution.py:260
  189.9 21.3 %reduce-scatter.21.cloned.1.call-done = bf16[240,1,768]{2,0,1:T(8,128)(2,1)} async-done(((bf16[960,1,768]{2,0,1:T(8,128)(2,1)}), bf16[240,1,768]{2,0,1:T(8,128)(2,1)}) %reduce-scatter.21.cloned.1.call-update) | async-done | bytes 368656 | tf_op jit(solution)/shard_map/reduce_scatter | solution.py:263
  211.3 35.5 %reduce-scatter.25.cloned.1.call-done = bf16[240,1,768]{2,0,1:T(8,128)(2,1)} async-done(((bf16[960,1,768]{2,0,1:T(8,128)(2,1)}), bf16[240,1,768]{2,0,1:T(8,128)(2,1)}) %reduce-scatter.25.cloned.1.call-update) | async-done | bytes 368656 | tf_op jit(solution)/shard_map/reduce_scatter | solution.py:263
  246.7 35.6 %reduce-scatter.29.cloned.1.call-done = bf16[240,1,768]{2,0,1:T(8,128)(2,1)} async-done(((bf16[960,1,768]{2,0,1:T(8,128)(2,1)}), bf16[240,1,768]{2,0,1:T(8,128)(2,1)}) %reduce-scatter.29.cloned.1.call-update) | async-done | bytes 368656 | tf_op jit(solution)/shard_map/reduce_scatter | solution.py:263
  282.3 35.0 %reduce-scatter.33.cloned.1.call-done = bf16[240,1,768]{2,0,1:T(8,128)(2,1)} async-done(((bf16[960,1,768]{2,0,1:T(8,128)(2,1)}), bf16[240,1,768]{2,0,1:T(8,128)(2,1)}) %reduce-scatter.33.cloned.1.call-update) | async-done | bytes 368656 | tf_op jit(solution)/shard_map/reduce_scatter | solution.py:263
  323.4 6.8 fusion.307
  345.2 11.7 all-gather.33.cloned.1.call-done
  361.6 31.1 %all-gather.47.cloned.1.call-done = bf16[960,1,768]{2,0,1:T(8,128)(2,1)} async-done(((bf16[240,1,768]{2,0,1:T(8,128)(2,1)}), bf16[960,1,768]{2,0,1:T(8,128)(2,1)}) %all-gather.47.cloned.1.call-update) | async-done | bytes 1474576 | tf_op jit(solution)/shard_map/all_gather | solution.py:282
  402.4 26.7 %all-gather.29.cloned.1.call-done = bf16[960,1,768]{2,0,1:T(8,128)(2,1)} async-done(((bf16[240,1,768]{2,0,1:T(8,128)(2,1)}), bf16[960,1,768]{2,0,1:T(8,128)(2,1)}) %all-gather.29.cloned.1.call-update) | async-done | bytes 1474576 | tf_op jit(solution)/shard_map/all_gather | solution.py:271
  433.8 31.1 %all-gather.43.cloned.1.call-done = bf16[960,1,768]{2,0,1:T(8,128)(2,1)} async-done(((bf16[240,1,768]{2,0,1:T(8,128)(2,1)}), bf16[960,1,768]{2,0,1:T(8,128)(2,1)}) %all-gather.43.cloned.1.call-update) | async-done | bytes 1474576 | tf_op jit(solution)/shard_map/all_gather | solution.py:282
  479.8 21.0 %all-gather.25.cloned.1.call-done = bf16[960,1,768]{2,0,1:T(8,128)(2,1)} async-done(((bf16[240,1,768]{2,0,1:T(8,128)(2,1)}), bf16[960,1,768]{2,0,1:T(8,128)(2,1)}) %all-gather.25.cloned.1.call-update) | async-done | bytes 1474576 | tf_op jit(solution)/shard_map/all_gather | solution.py:271
  505.4 31.1 %all-gather.39.cloned.1.call-done = bf16[960,1,768]{2,0,1:T(8,128)(2,1)} async-done(((bf16[240,1,768]{2,0,1:T(8,128)(2,1)}), bf16[960,1,768]{2,0,1:T(8,128)(2,1)}) %all-gather.39.cloned.1.call-update) | async-done | bytes 1474576 | tf_op jit(solution)/shard_map/all_gather | solution.py:282
  546.2 26.7 %all-gather.21.cloned.1.call-done = bf16[960,1,768]{2,0,1:T(8,128)(2,1)} async-done(((bf16[240,1,768]{2,0,1:T(8,128)(2,1)}), bf16[960,1,768]{2,0,1:T(8,128)(2,1)}) %all-gather.21.cloned.1.call-update) | async-done | bytes 1474576 | tf_op jit(solution)/shard_map/all_gather | solution.py:271
  577.5 31.1 %all-gather.35.cloned.1.call-done = bf16[960,1,768]{2,0,1:T(8,128)(2,1)} async-done(((bf16[240,1,768]{2,0,1:T(8,128)(2,1)}), bf16[960,1,768]{2,0,1:T(8,128)(2,1)}) %all-gather.35.cloned.1.call-update) | async-done | bytes 1474576 | tf_op jit(solution)/shard_map/all_gather | solution.py:282
  656.9 22.2 %reduce-scatter.45.cloned.1.call-done = bf16[240,1,768]{2,0,1:T(8,128)(2,1)} async-done(((bf16[960,1,768]{2,0,1:T(8,128)(2,1)}), bf16[240,1,768]{2,0,1:T(8,128)(2,1)}) %reduce-scatter.45.cloned.1.call-update) | async-done | bytes 368656 | tf_op jit(solution)/shard_map/reduce_scatter | solution.py:285
  683.7 31.0 %reduce-scatter.31.cloned.1.call-done = bf16[240,1,768]{2,0,1:T(8,128)(2,1)} async-done(((bf16[960,1,768]{2,0,1:T(8,128)(2,1)}), bf16[240,1,768]{2,0,1:T(8,128)(2,1)}) %reduce-scatter.31.cloned.1.call-update) | async-done | bytes 368656 | tf_op jit(solution)/shard_map/reduce_scatter | solution.py:274
  714.7 34.9 %reduce-scatter.41.cloned.1.call-done = bf16[240,1,768]{2,0,1:T(8,128)(2,1)} async-done(((bf16[960,1,768]{2,0,1:T(8,128)(2,1)}), bf16[240,1,768]{2,0,1:T(8,128)(2,1)}) %reduce-scatter.41.cloned.1.call-update) | async-done | bytes 368656 | tf_op jit(solution)/shard_map/reduce_scatter | solution.py:285
  749.6 35.6 %reduce-scatter.37.cloned.1.call-done = bf16[240,1,768]{2,0,1:T(8,128)(2,1)} async-done(((bf16[960,1,768]{2,0,1:T(8,128)(2,1)}), bf16[240,1,768]{2,0,1:T(8,128)(2,1)}) %reduce-scatter.37.cloned.1.call-update) | async-done | bytes 368656 | tf_op jit(solution)/shard_map/reduce_scatter | solution.py:285
  789.2 31.1 %reduce-scatter.35.cloned.1.call-done = bf16[240,1,768]{2,0,1:T(8,128)(2,1)} async-done(((bf16[960,1,768]{2,0,1:T(8,128)(2,1)}), bf16[240,1,768]{2,0,1:T(8,128)(2,1)}) %reduce-scatter.35.cloned.1.call-update) | async-done | bytes 368656 | tf_op jit(solution)/shard_map/reduce_scatter | solution.py:274
  823.7 31.5 %reduce-scatter.23.cloned.1.call-done = bf16[240,1,768]{2,0,1:T(8,128)(2,1)} async-done(((bf16[960,1,768]{2,0,1:T(8,128)(2,1)}), bf16[240,1,768]{2,0,1:T(8,128)(2,1)}) %reduce-scatter.23.cloned.1.call-update) | async-done | bytes 368656 | tf_op jit(solution)/shard_map/reduce_scatter | solution.py:274
  858.9 31.3 %reduce-scatter.27.cloned.1.call-done = bf16[240,1,768]{2,0,1:T(8,128)(2,1)} async-done(((bf16[960,1,768]{2,0,1:T(8,128)(2,1)}), bf16[240,1,768]{2,0,1:T(8,128)(2,1)}) %reduce-scatter.27.cloned.1.call-update) | async-done | bytes 368656 | tf_op jit(solution)/shard_map/reduce_scatter | solution.py:274
  897.5 37.2 %reduce-scatter.57.cloned.1.call-done = f32[96,768]{1,0:T(8,128)} async-done(((f32[768,768]{1,0:T(8,128)}), f32[96,768]{1,0:T(8,128)}) %reduce-scatter.57.cloned.1.call-update) | async-done | bytes 294928 | tf_op jit(solution)/shard_map/reduce_scatter | solution.py:330
  936.6 43.7 %reduce-scatter.59.cloned.1.call-done = f32[96,768]{1,0:T(8,128)} async-done(((f32[768,768]{1,0:T(8,128)}), f32[96,768]{1,0:T(8,128)}) %reduce-scatter.59.cloned.1.call-update) | async-done | bytes 294928 | tf_op jit(solution)/shard_map/reduce_scatter | solution.py:331
  982.2 35.5 %all-gather.41.cloned.1.call-done = bf16[960,1,768]{2,0,1:T(8,128)(2,1)} async-done(((bf16[240,1,768]{2,0,1:T(8,128)(2,1)}), bf16[960,1,768]{2,0,1:T(8,128)(2,1)}) %all-gather.41.cloned.1.call-update) | async-done | bytes 1474576 | tf_op jit(solution)/shard_map/all_gather | solution.py:293
  1019.7 10.1 multiply_reduce_fusion.2
  1032.0 6.5 multiply_convert_fusion.2
  1042.4 11.8 all-gather.49.cloned.1.call-done
  1056.2 9.9 multiply_reduce_fusion
  1080.5 10.1 all-gather.45.cloned.1.call-done
  1092.6 9.9 multiply_reduce_fusion.1
  1104.7 6.6 multiply_convert_fusion.1
  1115.9 10.4 all-gather.37.cloned.1.call-done
  1134.7 8.5 multiply_reduce_fusion.3
  1143.2 7.0 multiply_convert_fusion.3
  1158.8 6.5 fusion.10
  1206.2 13.7 all-reduce.1
  1226.7 8.5 all_gather.77
  1236.2 24.4 %reduce-scatter.53.cloned.1.call-done = f32[96,3,192]{2,0,1:T(8,128)} async-done(((f32[768,3,192]{2,0,1:T(8,128)}), f32[96,3,192]{2,0,1:T(8,128)}) %reduce-scatter.53.cloned.1.call-update) | async-done | bytes 221200 | tf_op jit(solution)/shard_map/reduce_scatter | solution.py:328
  1261.6 12.1 all_gather.76
  1276.2 20.6 %reduce-scatter.51.cloned.1.call-done = bf16[240,1,768]{2,0,1:T(8,128)(2,1)} async-done(((bf16[960,1,768]{2,0,1:T(8,128)(2,1)}), bf16[240,1,768]{2,0,1:T(8,128)(2,1)}) %reduce-scatter.51.cloned.1.call-update) | async-done | bytes 368656 | tf_op jit(solution)/shard_map/reduce_scatter | solution.py:296
  1298.2 33.5 %reduce-scatter.43.cloned.1.call-done = bf16[240,1,768]{2,0,1:T(8,128)(2,1)} async-done(((bf16[960,1,768]{2,0,1:T(8,128)(2,1)}), bf16[240,1,768]{2,0,1:T(8,128)(2,1)}) %reduce-scatter.43.cloned.1.call-update) | async-done | bytes 368656 | tf_op jit(solution)/shard_map/reduce_scatter | solution.py:296
  1331.8 34.9 %reduce-scatter.47.cloned.1.call-done = bf16[240,1,768]{2,0,1:T(8,128)(2,1)} async-done(((bf16[960,1,768]{2,0,1:T(8,128)(2,1)}), bf16[240,1,768]{2,0,1:T(8,128)(2,1)}) %reduce-scatter.47.cloned.1.call-update) | async-done | bytes 368656 | tf_op jit(solution)/shard_map/reduce_scatter | solution.py:296
  1366.6 35.6 %reduce-scatter.39.cloned.1.call-done = bf16[240,1,768]{2,0,1:T(8,128)(2,1)} async-done(((bf16[960,1,768]{2,0,1:T(8,128)(2,1)}), bf16[240,1,768]{2,0,1:T(8,128)(2,1)}) %reduce-scatter.39.cloned.1.call-update) | async-done | bytes 368656 | tf_op jit(solution)/shard_map/reduce_scatter | solution.py:296
  1411.2 40.3 %all-reduce = (f32[768]{0:T(1024)}, f32[768]{0:T(1024)}, f32[768]{0:T(1024)}, f32[768]{0:T(1024)}, f32[768]{0:T(1024)}, /*index=5*/f32[768]{0:T(1024)}, f32[5,768]{1,0:T(8,128)}) all-reduce(f32[768]{0:T(1024)S(1)} %add_add_fusion.33, f32[768]{0:T(1024)S(1)} %add_add_fusion.31, ...), channel_id=1, replica_groups=mesh['batch'=8,'tensor'=4] {'batch','tensor'}, use_global_device_ids=true, to_apply=%region_82.84 | all-reduce | flops 8448 | bytes 67584 | tf_op jit(solution)/shard_map/psum | solution.py:352
  (676 shorter events, 330.1 us)
Async XLA Ops:
  7.2 385.5 %copy-start = (bf16[768,768]{1,0:T(8,128)(2,1)S(1)}, bf16[768,768]{1,0:T(8,128)(2,1)}, u32[]{:S(2)}) copy-start(bf16[768,768]{1,0:T(8,128)(2,1)} %param.28) | copy-start | bytes 3538948
  7.2 59.7 %all-gather.19.cloned.1.call-start = ((), (), s32[]{:S(2)}) async-start(), calls=%async_computation.20 | async-start | bytes 1843200 | tf_op jit(solution)/shard_map/all_gather | solution.py:260
  28.7 74.7 %all-gather.23.cloned.1.call-start = ((), (), s32[]{:S(2)}) async-start(), calls=%async_computation.24 | async-start | bytes 1843200 | tf_op jit(solution)/shard_map/all_gather | solution.py:260
  29.5 110.4 %all-gather.27.cloned.1.call-start = ((), (), s32[]{:S(2)}) async-start(), calls=%async_computation.28 | async-start | bytes 1843200 | tf_op jit(solution)/shard_map/all_gather | solution.py:260
  30.2 145.4 %all-gather.31.cloned.1.call-start = ((), (), s32[]{:S(2)}) async-start(), calls=%async_computation.32 | async-start | bytes 1843200 | tf_op jit(solution)/shard_map/all_gather | solution.py:260
  30.8 180.4 %reduce-scatter.21.cloned.1.call-start = ((), (), s32[]{:S(2)}) async-start(), calls=%async_computation.21 | async-start | bytes 1843200 | tf_op jit(solution)/shard_map/reduce_scatter | solution.py:263
  33.9 985.7 %copy-start.98 = (f32[3,64]{1,0:T(4,128)}, f32[3,64]{1,0:T(4,128)S(1)}, u32[]{:S(2)}) copy-start(f32[3,64]{1,0:T(4,128)S(1)} %reshape.2253) | copy-start | bytes 2308
  81.6 165.2 %reduce-scatter.25.cloned.1.call-start = ((), (), s32[]{:S(2)}) async-start(), calls=%async_computation.25 | async-start | bytes 1843200 | tf_op jit(solution)/shard_map/reduce_scatter | solution.py:263
  118.0 164.3 %reduce-scatter.29.cloned.1.call-start = ((), (), s32[]{:S(2)}) async-start(), calls=%async_computation.29 | async-start | bytes 1843200 | tf_op jit(solution)/shard_map/reduce_scatter | solution.py:263
  154.2 163.2 %reduce-scatter.33.cloned.1.call-start = ((), (), s32[]{:S(2)}) async-start(), calls=%async_computation.33 | async-start | bytes 1843200 | tf_op jit(solution)/shard_map/reduce_scatter | solution.py:263
  189.8 167.1 %all-gather.33.cloned.1.call-start = ((), (), s32[]{:S(2)}) async-start(), calls=%async_computation.34 | async-start | bytes 1843200 | tf_op jit(solution)/shard_map/all_gather | solution.py:271
  322.7 70.0 %all-gather.47.cloned.1.call-start = ((), (), s32[]{:S(2)}) async-start(), calls=%async_computation.48 | async-start | bytes 1843200 | tf_op jit(solution)/shard_map/all_gather | solution.py:282
  332.6 96.5 %all-gather.29.cloned.1.call-start = ((), (), s32[]{:S(2)}) async-start(), calls=%async_computation.30 | async-start | bytes 1843200 | tf_op jit(solution)/shard_map/all_gather | solution.py:271
  333.3 131.6 %all-gather.43.cloned.1.call-start = ((), (), s32[]{:S(2)}) async-start(), calls=%async_computation.44 | async-start | bytes 1843200 | tf_op jit(solution)/shard_map/all_gather | solution.py:282
  336.7 164.1 %all-gather.25.cloned.1.call-start = ((), (), s32[]{:S(2)}) async-start(), calls=%async_computation.26 | async-start | bytes 1843200 | tf_op jit(solution)/shard_map/all_gather | solution.py:271
  337.4 199.1 %all-gather.39.cloned.1.call-start = ((), (), s32[]{:S(2)}) async-start(), calls=%async_computation.40 | async-start | bytes 1843200 | tf_op jit(solution)/shard_map/all_gather | solution.py:282
  340.8 232.0 %all-gather.21.cloned.1.call-start = ((), (), s32[]{:S(2)}) async-start(), calls=%async_computation.22 | async-start | bytes 1843200 | tf_op jit(solution)/shard_map/all_gather | solution.py:271
  341.4 267.2 %all-gather.35.cloned.1.call-start = ((), (), s32[]{:S(2)}) async-start(), calls=%async_computation.36 | async-start | bytes 1843200 | tf_op jit(solution)/shard_map/all_gather | solution.py:282
  344.7 312.2 %reduce-scatter.49.cloned.1.call-start = ((), (), s32[]{:S(2)}) async-start(), calls=%async_computation.49 | async-start | bytes 1843200 | tf_op jit(solution)/shard_map/reduce_scatter | solution.py:285
  402.3 276.8 %reduce-scatter.45.cloned.1.call-start = ((), (), s32[]{:S(2)}) async-start(), calls=%async_computation.45 | async-start | bytes 1843200 | tf_op jit(solution)/shard_map/reduce_scatter | solution.py:285
  474.5 240.2 %reduce-scatter.31.cloned.1.call-start = ((), (), s32[]{:S(2)}) async-start(), calls=%async_computation.31 | async-start | bytes 1843200 | tf_op jit(solution)/shard_map/reduce_scatter | solution.py:274
  479.5 270.1 %reduce-scatter.41.cloned.1.call-start = ((), (), s32[]{:S(2)}) async-start(), calls=%async_computation.41 | async-start | bytes 1843200 | tf_op jit(solution)/shard_map/reduce_scatter | solution.py:285
  546.1 239.1 %reduce-scatter.37.cloned.1.call-start = ((), (), s32[]{:S(2)}) async-start(), calls=%async_computation.37 | async-start | bytes 1843200 | tf_op jit(solution)/shard_map/reduce_scatter | solution.py:285
  618.2 202.0 %reduce-scatter.35.cloned.1.call-start = ((), (), s32[]{:S(2)}) async-start(), calls=%async_computation.35 | async-start | bytes 1843200 | tf_op jit(solution)/shard_map/reduce_scatter | solution.py:274
  623.2 232.1 %reduce-scatter.23.cloned.1.call-start = ((), (), s32[]{:S(2)}) async-start(), calls=%async_computation.23 | async-start | bytes 1843200 | tf_op jit(solution)/shard_map/reduce_scatter | solution.py:274
  628.3 261.9 %reduce-scatter.27.cloned.1.call-start = ((), (), s32[]{:S(2)}) async-start(), calls=%async_computation.27 | async-start | bytes 1843200 | tf_op jit(solution)/shard_map/reduce_scatter | solution.py:274
  633.6 301.1 %reduce-scatter.57.cloned.1.call-start = ((), (), s32[]{:S(2)}) async-start(), calls=%async_computation.56 | async-start | bytes 2654208 | tf_op jit(solution)/shard_map/reduce_scatter | solution.py:330
  643.9 336.4 %reduce-scatter.59.cloned.1.call-start = ((), (), s32[]{:S(2)}) async-start(), calls=%async_computation.57 | async-start | bytes 2654208 | tf_op jit(solution)/shard_map/reduce_scatter | solution.py:331
  656.9 360.8 %all-gather.41.cloned.1.call-start = ((), (), s32[]{:S(2)}) async-start(), calls=%async_computation.42 | async-start | bytes 1843200 | tf_op jit(solution)/shard_map/all_gather | solution.py:293
  894.9 159.3 %all-gather.49.cloned.1.call-start = ((), (), s32[]{:S(2)}) async-start(), calls=%async_computation.50 | async-start | bytes 1843200 | tf_op jit(solution)/shard_map/all_gather | solution.py:293
  895.7 194.9 %all-gather.45.cloned.1.call-start = ((), (), s32[]{:S(2)}) async-start(), calls=%async_computation.46 | async-start | bytes 1843200 | tf_op jit(solution)/shard_map/all_gather | solution.py:293
  896.6 229.7 %all-gather.37.cloned.1.call-start = ((), (), s32[]{:S(2)}) async-start(), calls=%async_computation.38 | async-start | bytes 1843200 | tf_op jit(solution)/shard_map/all_gather | solution.py:293
  897.4 322.5 %all-gather.51.cloned.1.call-start = ((), (), s32[]{:S(2)}) async-start(), calls=%async_computation.52 | async-start | bytes 1327104 | tf_op jit(solution)/shard_map/all_gather | solution.py:345
  936.4 286.4 %all-gather.53.cloned.1.call-start = ((), (), s32[]{:S(2)}) async-start(), calls=%async_computation.53 | async-start | bytes 1327104 | tf_op jit(solution)/shard_map/all_gather | solution.py:348
  982.0 243.8 %reduce-scatter.55.cloned.1.call-start = ((), (), s32[]{:S(2)}) async-start(), calls=%async_computation.55 | async-start | bytes 663552 | tf_op jit(solution)/shard_map/reduce_scatter | solution.py:329
  1173.6 87.0 %reduce-scatter.53.cloned.1.call-start = ((), (), s32[]{:S(2)}) async-start(), calls=%async_computation.54 | async-start | bytes 2654208 | tf_op jit(solution)/shard_map/reduce_scatter | solution.py:328
  1184.9 112.0 %reduce-scatter.51.cloned.1.call-start = ((), (), s32[]{:S(2)}) async-start(), calls=%async_computation.51 | async-start | bytes 1843200 | tf_op jit(solution)/shard_map/reduce_scatter | solution.py:296
  1188.6 143.1 %reduce-scatter.43.cloned.1.call-start = ((), (), s32[]{:S(2)}) async-start(), calls=%async_computation.43 | async-start | bytes 1843200 | tf_op jit(solution)/shard_map/reduce_scatter | solution.py:296
  1192.9 173.8 %reduce-scatter.47.cloned.1.call-start = ((), (), s32[]{:S(2)}) async-start(), calls=%async_computation.47 | async-start | bytes 1843200 | tf_op jit(solution)/shard_map/reduce_scatter | solution.py:296
  1196.6 205.7 %reduce-scatter.39.cloned.1.call-start = ((), (), s32[]{:S(2)}) async-start(), calls=%async_computation.39 | async-start | bytes 1843200 | tf_op jit(solution)/shard_map/reduce_scatter | solution.py:296
  1236.1 166.1 %copy-start.9 = (f32[240,1,768]{2,0,1:T(8,128)S(1)}, f32[240,1,768]{2,0,1:T(8,128)}, u32[]{:S(2)}) copy-start(f32[240,1,768]{2,0,1:T(8,128)} %copy-done.8) | copy-start | bytes 2211844
  1236.1 166.1 %copy-start.11 = (f32[240,1,768]{2,0,1:T(8,128)S(1)}, f32[240,1,768]{2,0,1:T(8,128)}, u32[]{:S(2)}) copy-start(f32[240,1,768]{2,0,1:T(8,128)} %copy-done.10) | copy-start | bytes 2211844
  1236.1 166.2 %copy-start.13 = (f32[240,1,768]{2,0,1:T(8,128)S(1)}, f32[240,1,768]{2,0,1:T(8,128)}, u32[]{:S(2)}) copy-start(f32[240,1,768]{2,0,1:T(8,128)} %copy-done.12) | copy-start | bytes 2211844
  1236.1 166.1 %copy-start.103 = (f32[240]{0:T(256)S(1)}, f32[240]{0:T(256)}, u32[]{:S(2)}) copy-start(f32[240]{0:T(256)} %copy-done.102) | copy-start | bytes 2884
  1236.1 166.1 %copy-start.105 = (f32[240]{0:T(256)S(1)}, f32[240]{0:T(256)}, u32[]{:S(2)}) copy-start(f32[240]{0:T(256)} %copy-done.104) | copy-start | bytes 2884
  1236.1 166.1 %copy-start.107 = (f32[240]{0:T(256)S(1)}, f32[240]{0:T(256)}, u32[]{:S(2)}) copy-start(f32[240]{0:T(256)} %copy-done.106) | copy-start | bytes 2884
  1236.1 166.1 %copy-start.127 = (f32[240]{0:T(256)S(1)}, f32[240]{0:T(256)}, u32[]{:S(2)}) copy-start(f32[240]{0:T(256)} %copy-done.126) | copy-start | bytes 2884
  1236.2 166.1 %copy-start.129 = (f32[240]{0:T(256)S(1)}, f32[240]{0:T(256)}, u32[]{:S(2)}) copy-start(f32[240]{0:T(256)} %copy-done.128) | copy-start | bytes 2884
  (185 other events, 2812.5 us)
Sparse Core Ops, SparseCore 0:
  28.8 38.0 all-gather.18
  69.1 34.2 all-gather.22
  105.5 34.2 all-gather.26
  141.3 34.2 all-gather.30
  178.4 32.8 reduce-scatter.20
  214.0 32.6 reduce-scatter.24
  249.6 32.6 reduce-scatter.28
  284.7 32.6 reduce-scatter.32
  322.8 34.0 all-gather.32
  358.3 34.2 all-gather.46
  394.8 34.2 all-gather.28
  430.6 34.2 all-gather.42
  466.4 34.2 all-gather.24
  502.2 34.2 all-gather.38
  538.5 34.2 all-gather.20
  574.3 34.2 all-gather.34
  610.7 32.8 reduce-scatter.48
  646.4 32.6 reduce-scatter.44
  682.0 32.6 reduce-scatter.30
  716.9 32.6 reduce-scatter.40
  752.5 32.6 reduce-scatter.36
  787.5 32.6 reduce-scatter.34
  822.6 32.6 reduce-scatter.22
  857.5 32.6 reduce-scatter.26
  893.5 41.1 reduce-scatter.56
  937.9 42.3 reduce-scatter.58
  982.3 35.3 all-gather.40
  1019.8 34.2 all-gather.48
  1056.3 34.2 all-gather.44
  1092.0 34.2 all-gather.36
  1128.2 22.8 all-gather.50
  1153.0 23.9 all-gather.52
  1180.5 34.3 reduce-scatter.54
  1218.3 42.2 reduce-scatter.52
  1262.9 33.9 reduce-scatter.50
  1299.0 32.6 reduce-scatter.42
  1333.9 32.6 reduce-scatter.46
  1369.5 32.6 reduce-scatter.38
where the time goes:
time: 1460 us
  waiting for transfers between devices  952 us (65%)
  matrix products  246 us (17%)
  other arithmetic  98.3 us (7%)
  blocking collectives  74.7 us (5%)
  local copies, waits for them, and re-layouts  56.1 us (4%)
  between operations  27.5 us (2%)
    reduce_scatter x4, waiting for transfers between devices, sum_attn(): lax.psum_scatter(term(jnp.int32(0), lax.axis_size('tensor') * rows).astyp...  127 us
    reduce_scatter x4, waiting for transfers between devices, sum_mlp(): lax.psum_scatter(term(jnp.int32(0), lax.axis_size('tensor') * rows).astyp...  125 us
    reduce_scatter x4, waiting for transfers between devices, sum_qkv(): lax.psum_scatter(term(jnp.int32(0), lax.axis_size('tensor') * rows).astyp...  125 us
    all_gather x4, waiting for transfers between devices, gather_grad(): return lax.all_gather(values, 'tensor', axis=0, tiled=True)  124 us
    all_gather x4, waiting for transfers between devices, gather_first(): return lax.all_gather(values, 'tensor', axis=0, tiled=True)  93.8 us
    reduce_scatter x4, waiting for transfers between devices, sum_upward(): lax.psum_scatter(term(jnp.int32(0), lax.axis_size('tensor') * rows).astyp...  92.7 us
    all_gather x4, waiting for transfers between devices, gather_second(): return lax.all_gather(values, 'tensor', axis=0, tiled=True)  86.1 us
    all_gather x4, waiting for transfers between devices, gather_attn(): return lax.all_gather(values, 'tensor', axis=0, tiled=True)  67.8 us
  transfers between devices with their start and end apart: 38, of which 34 were waited for; matrix products, arithmetic and copies ran while one was open for 23% of the time, Pallas kernels for 0%

commit v1 on v0

--- a/solution.py
+++ b/solution.py
@@ -12,6 +12,19 @@
 HIGHEST = lax.Precision.HIGHEST
 EPSILON = 1e-05
 MASKED = -1e30
+
+
+def collect(x, axis, dim):
+    ways = lax.axis_size(axis)
+    up = [(d, (d + 1) % ways) for d in range(ways)]
+    down = [(d, (d - 1) % ways) for d in range(ways)]
+    earlier, later = ([x], [x])
+    for _ in range(ways // 2):
+        earlier.append(lax.ppermute(earlier[-1], axis, up))
+    for _ in range((ways - 1) // 2):
+        later.append(lax.ppermute(later[-1], axis, down))
+    line = jnp.concatenate([*earlier[::-1], *later[1:]], axis=dim)
+    return jnp.roll(line, (lax.axis_index(axis) - ways // 2) * x.shape[dim], axis=dim)
 
 
 def norm_rows(values, gain, shift):
@@ -290,7 +303,7 @@
         ).astype(jnp.float32)
 
     def gather_attn(values):
-        return lax.all_gather(values, "tensor", axis=0, tiled=True)
+        return collect(values, "tensor", 0)
 
     def sum_qkv(term):
         return lax.psum_scatter(

time: 1460 us -> 1380 us (0.945)
  waiting for transfers between devices: 952 us -> 831 us
  other arithmetic: 98.3 us -> 136 us
  starting transfers between devices: 4.51 us -> 20.6 us
  matrix products: 246 us -> 231 us
    all_gather x4 -> x0, waiting for transfers between devices: 67.8 us -> none  [gather_attn(): return lax.all_gather(values, 'tensor', axis=0, tiled=True)]
    reduce_scatter x1, waiting for transfers between devices: 43.7 us -> 1.6 us  [per_device(): lax.psum_scatter(matrices[3], 'batch', scatter_dimension=0, tiled=True)]
    reduce_scatter x1, waiting for transfers between devices: 37.2 us -> 0.02 us  [per_device(): lax.psum_scatter(matrices[2], 'batch', scatter_dimension=0, tiled=True)]
    another operation x0 -> x4, other arithmetic: none -> 34.9 us
    ppermute x0 -> x12, waiting for transfers between devices: none -> 33.9 us  [the longest x8 33.2 us: collect(): earlier.append(lax.ppermute(earlier[-1], axis, up))]
    reduce_scatter x4, waiting for transfers between devices: 125 us -> 150 us  [sum_mlp(): lax.psum_scatter(term(jnp.int32(0), lax.axis_size('tensor') * rows).astyp...]
    reduce_scatter x1, waiting for transfers between devices: 24.4 us -> 0.02 us  [per_device(): lax.psum_scatter(matrices[0], 'batch', scatter_dimension=0, tiled=True)]
    ppermute x0 -> x12, starting transfers between devices: none -> 17 us  [the longest x4 9.7 us: collect(): later.append(lax.ppermute(later[-1], axis, down))]
  transfers between devices with their start and end apart: 38 -> 46, of which waited for: 34 -> 33; matrix products, arithmetic and copies ran while one was open for 23% -> 26% of each run, Pallas kernels for 0% -> 0%
where the time goes in v1:
time: 1380 us; the launch traced here: 1370 us
  waiting for transfers between devices  831 us (60%)
  matrix products  231 us (17%)
  other arithmetic  136 us (10%)
  blocking collectives  76.9 us (6%)
  local copies, waits for them, and re-layouts  50.4 us (4%)
  between operations  27.9 us (2%)
  starting transfers between devices  20.6 us (1%)
    reduce_scatter x4, waiting for transfers between devices, sum_mlp(): lax.psum_scatter(term(jnp.int32(0), lax.axis_size('tensor') * rows).astyp...  150 us
    reduce_scatter x4, waiting for transfers between devices, sum_attn(): lax.psum_scatter(term(jnp.int32(0), lax.axis_size('tensor') * rows).astyp...  128 us
    all_gather x4, waiting for transfers between devices, gather_grad(): return lax.all_gather(values, 'tensor', axis=0, tiled=True)  125 us
    reduce_scatter x4, waiting for transfers between devices, sum_qkv(): lax.psum_scatter(term(jnp.int32(0), lax.axis_size('tensor') * rows).astyp...  116 us
    all_gather x4, waiting for transfers between devices, gather_first(): return lax.all_gather(values, 'tensor', axis=0, tiled=True)  93.8 us
    reduce_scatter x4, waiting for transfers between devices, sum_upward(): lax.psum_scatter(term(jnp.int32(0), lax.axis_size('tensor') * rows).astyp...  92.8 us
    all_gather x4, waiting for transfers between devices, gather_second(): return lax.all_gather(values, 'tensor', axis=0, tiled=True)  86.5 us
    psum x1, blocking collectives, per_device(): lax.psum((shared_totals[0], shared_totals[1], shared_totals[2], shared_to...  40.3 us
  transfers between devices with their start and end apart: 46, of which 33 were waited for; matrix products, arithmetic and copies ran while one was open for 26% of the time, Pallas kernels for 0%

profile of v1, /device:TPU:0, one launch (start us, length us, event | category | flops | bytes accessed | tf_op | source)
XLA Modules:
  0.0 1374.1 jit_solution(10053224566722302420)
XLA Ops:
  15.2 6.8 fusion.305
  37.1 29.8 %all-gather.15.cloned.1.call-done = bf16[960,1,768]{2,0,1:T(8,128)(2,1)} async-done(((bf16[240,1,768]{2,0,1:T(8,128)(2,1)}), bf16[960,1,768]{2,0,1:T(8,128)(2,1)}) %all-gather.15.cloned.1.call-update) | async-done | bytes 1474576 | tf_op jit(solution)/shard_map/all_gather | solution.py:273
  81.8 21.6 %all-gather.19.cloned.1.call-done = bf16[960,1,768]{2,0,1:T(8,128)(2,1)} async-done(((bf16[240,1,768]{2,0,1:T(8,128)(2,1)}), bf16[960,1,768]{2,0,1:T(8,128)(2,1)}) %all-gather.19.cloned.1.call-update) | async-done | bytes 1474576 | tf_op jit(solution)/shard_map/all_gather | solution.py:273
  118.3 21.6 %all-gather.23.cloned.1.call-done = bf16[960,1,768]{2,0,1:T(8,128)(2,1)} async-done(((bf16[240,1,768]{2,0,1:T(8,128)(2,1)}), bf16[960,1,768]{2,0,1:T(8,128)(2,1)}) %all-gather.23.cloned.1.call-update) | async-done | bytes 1474576 | tf_op jit(solution)/shard_map/all_gather | solution.py:273
  154.7 20.9 %all-gather.27.cloned.1.call-done = bf16[960,1,768]{2,0,1:T(8,128)(2,1)} async-done(((bf16[240,1,768]{2,0,1:T(8,128)(2,1)}), bf16[960,1,768]{2,0,1:T(8,128)(2,1)}) %all-gather.27.cloned.1.call-update) | async-done | bytes 1474576 | tf_op jit(solution)/shard_map/all_gather | solution.py:273
  189.8 21.4 %reduce-scatter.21.cloned.1.call-done = bf16[240,1,768]{2,0,1:T(8,128)(2,1)} async-done(((bf16[960,1,768]{2,0,1:T(8,128)(2,1)}), bf16[240,1,768]{2,0,1:T(8,128)(2,1)}) %reduce-scatter.21.cloned.1.call-update) | async-done | bytes 368656 | tf_op jit(solution)/shard_map/reduce_scatter | solution.py:276
  211.2 35.5 %reduce-scatter.25.cloned.1.call-done = bf16[240,1,768]{2,0,1:T(8,128)(2,1)} async-done(((bf16[960,1,768]{2,0,1:T(8,128)(2,1)}), bf16[240,1,768]{2,0,1:T(8,128)(2,1)}) %reduce-scatter.25.cloned.1.call-update) | async-done | bytes 368656 | tf_op jit(solution)/shard_map/reduce_scatter | solution.py:276
  246.7 35.6 %reduce-scatter.29.cloned.1.call-done = bf16[240,1,768]{2,0,1:T(8,128)(2,1)} async-done(((bf16[960,1,768]{2,0,1:T(8,128)(2,1)}), bf16[240,1,768]{2,0,1:T(8,128)(2,1)}) %reduce-scatter.29.cloned.1.call-update) | async-done | bytes 368656 | tf_op jit(solution)/shard_map/reduce_scatter | solution.py:276
  282.3 35.0 %reduce-scatter.33.cloned.1.call-done = bf16[240,1,768]{2,0,1:T(8,128)(2,1)} async-done(((bf16[960,1,768]{2,0,1:T(8,128)(2,1)}), bf16[240,1,768]{2,0,1:T(8,128)(2,1)}) %reduce-scatter.33.cloned.1.call-update) | async-done | bytes 368656 | tf_op jit(solution)/shard_map/reduce_scatter | solution.py:276
  323.4 6.8 fusion.304
  344.9 12.1 all-gather.29.cloned.1.call-done
  361.6 31.1 %all-gather.37.cloned.1.call-done = bf16[960,1,768]{2,0,1:T(8,128)(2,1)} async-done(((bf16[240,1,768]{2,0,1:T(8,128)(2,1)}), bf16[960,1,768]{2,0,1:T(8,128)(2,1)}) %all-gather.37.cloned.1.call-update) | async-done | bytes 1474576 | tf_op jit(solution)/shard_map/all_gather | solution.py:295
  402.3 26.8 %all-gather.25.cloned.1.call-done = bf16[960,1,768]{2,0,1:T(8,128)(2,1)} async-done(((bf16[240,1,768]{2,0,1:T(8,128)(2,1)}), bf16[960,1,768]{2,0,1:T(8,128)(2,1)}) %all-gather.25.cloned.1.call-update) | async-done | bytes 1474576 | tf_op jit(solution)/shard_map/all_gather | solution.py:284
  433.7 31.2 %all-gather.35.cloned.1.call-done = bf16[960,1,768]{2,0,1:T(8,128)(2,1)} async-done(((bf16[240,1,768]{2,0,1:T(8,128)(2,1)}), bf16[960,1,768]{2,0,1:T(8,128)(2,1)}) %all-gather.35.cloned.1.call-update) | async-done | bytes 1474576 | tf_op jit(solution)/shard_map/all_gather | solution.py:295
  479.8 21.0 %all-gather.21.cloned.1.call-done = bf16[960,1,768]{2,0,1:T(8,128)(2,1)} async-done(((bf16[240,1,768]{2,0,1:T(8,128)(2,1)}), bf16[960,1,768]{2,0,1:T(8,128)(2,1)}) %all-gather.21.cloned.1.call-update) | async-done | bytes 1474576 | tf_op jit(solution)/shard_map/all_gather | solution.py:284
  505.3 31.2 %all-gather.33.cloned.1.call-done = bf16[960,1,768]{2,0,1:T(8,128)(2,1)} async-done(((bf16[240,1,768]{2,0,1:T(8,128)(2,1)}), bf16[960,1,768]{2,0,1:T(8,128)(2,1)}) %all-gather.33.cloned.1.call-update) | async-done | bytes 1474576 | tf_op jit(solution)/shard_map/all_gather | solution.py:295
  536.5 6.0 convert_reduce_fusion.2
  546.2 26.6 %all-gather.17.cloned.1.call-done = bf16[960,1,768]{2,0,1:T(8,128)(2,1)} async-done(((bf16[240,1,768]{2,0,1:T(8,128)(2,1)}), bf16[960,1,768]{2,0,1:T(8,128)(2,1)}) %all-gather.17.cloned.1.call-update) | async-done | bytes 1474576 | tf_op jit(solution)/shard_map/all_gather | solution.py:284
  577.5 31.1 %all-gather.31.cloned.1.call-done = bf16[960,1,768]{2,0,1:T(8,128)(2,1)} async-done(((bf16[240,1,768]{2,0,1:T(8,128)(2,1)}), bf16[960,1,768]{2,0,1:T(8,128)(2,1)}) %all-gather.31.cloned.1.call-update) | async-done | bytes 1474576 | tf_op jit(solution)/shard_map/all_gather | solution.py:295
  656.8 22.2 %reduce-scatter.45.cloned.1.call-done = bf16[240,1,768]{2,0,1:T(8,128)(2,1)} async-done(((bf16[960,1,768]{2,0,1:T(8,128)(2,1)}), bf16[240,1,768]{2,0,1:T(8,128)(2,1)}) %reduce-scatter.45.cloned.1.call-update) | async-done | bytes 368656 | tf_op jit(solution)/shard_map/reduce_scatter | solution.py:298
  682.6 32.1 %reduce-scatter.31.cloned.1.call-done = bf16[240,1,768]{2,0,1:T(8,128)(2,1)} async-done(((bf16[960,1,768]{2,0,1:T(8,128)(2,1)}), bf16[240,1,768]{2,0,1:T(8,128)(2,1)}) %reduce-scatter.31.cloned.1.call-update) | async-done | bytes 368656 | tf_op jit(solution)/shard_map/reduce_scatter | solution.py:287
  714.7 34.9 %reduce-scatter.41.cloned.1.call-done = bf16[240,1,768]{2,0,1:T(8,128)(2,1)} async-done(((bf16[960,1,768]{2,0,1:T(8,128)(2,1)}), bf16[240,1,768]{2,0,1:T(8,128)(2,1)}) %reduce-scatter.41.cloned.1.call-update) | async-done | bytes 368656 | tf_op jit(solution)/shard_map/reduce_scatter | solution.py:298
  749.6 35.6 %reduce-scatter.37.cloned.1.call-done = bf16[240,1,768]{2,0,1:T(8,128)(2,1)} async-done(((bf16[960,1,768]{2,0,1:T(8,128)(2,1)}), bf16[240,1,768]{2,0,1:T(8,128)(2,1)}) %reduce-scatter.37.cloned.1.call-update) | async-done | bytes 368656 | tf_op jit(solution)/shard_map/reduce_scatter | solution.py:298
  791.9 40.8 %reduce-scatter.35.cloned.1.call-done = bf16[240,1,768]{2,0,1:T(8,128)(2,1)} async-done(((bf16[960,1,768]{2,0,1:T(8,128)(2,1)}), bf16[240,1,768]{2,0,1:T(8,128)(2,1)}) %reduce-scatter.35.cloned.1.call-update) | async-done | bytes 368656 | tf_op jit(solution)/shard_map/reduce_scatter | solution.py:287
  840.2 40.8 %reduce-scatter.23.cloned.1.call-done = bf16[240,1,768]{2,0,1:T(8,128)(2,1)} async-done(((bf16[960,1,768]{2,0,1:T(8,128)(2,1)}), bf16[240,1,768]{2,0,1:T(8,128)(2,1)}) %reduce-scatter.23.cloned.1.call-update) | async-done | bytes 368656 | tf_op jit(solution)/shard_map/reduce_scatter | solution.py:287
  885.4 36.6 %reduce-scatter.27.cloned.1.call-done = bf16[240,1,768]{2,0,1:T(8,128)(2,1)} async-done(((bf16[960,1,768]{2,0,1:T(8,128)(2,1)}), bf16[240,1,768]{2,0,1:T(8,128)(2,1)}) %reduce-scatter.27.cloned.1.call-update) | async-done | bytes 368656 | tf_op jit(solution)/shard_map/reduce_scatter | solution.py:287
  946.6 6.3 collective-permute-done.3
  954.5 6.2 collective-permute-done.10
  960.7 7.1 fusion.60
  968.5 15.0 %collective-permute-done.4 = bf16[240,1,768]{2,0,1:T(8,128)(2,1)S(1)} collective-permute-done((bf16[240,1,768]{2,0,1:T(8,128)(2,1)S(1)}, bf16[240,1,768]{2,0,1:T(8,128)(2,1)S(1)}, u32[]{:S(2)}, u32[]{:S(2)}) %collective-permute-start.4) | collective-permute-done | bytes 368672 | tf_op jit(solution)/shard_map/ppermute | solution.py:23
  983.5 10.7 fusion.76
  995.2 11.2 fusion.84
  1019.5 6.5 fusion.10
  1026.0 10.3 multiply_reduce_fusion.1
  1036.4 10.0 multiply_convert_fusion.1
  1057.8 6.5 multiply_reduce_fusion
  1064.3 9.5 multiply_convert_fusion
  1083.1 6.5 multiply_reduce_fusion.2
  1089.6 9.3 multiply_convert_fusion.2
  1112.5 6.8 multiply_convert_fusion.3
  1153.1 14.1 %all-reduce.1 = (f32[192]{0:T(256)}, f32[192]{0:T(256)}, f32[768]{0:T(1024)}) all-reduce(f32[192]{0:T(256)S(1)} %add_add_fusion.35, f32[192]{0:T(256)S(1)} %add_add_fusion.34, f32[768]{0:T(1024)S(1)} %add_add_fusion.32), channel_id=1, replica_groups=mesh['batch'=8,'tensor'=4] {'batch'}, use_global_device_ids=true, to_apply=%region_68.71 | all-reduce | flops 1152 | bytes 9216 | tf_op jit(solution)/shard_map/psum | solution.py:377
  1168.0 9.9 all_gather.61
  1185.7 12.7 all_gather.60
  1200.9 11.4 reduce-scatter.51.cloned.1.call-done
  1213.6 33.7 %reduce-scatter.47.cloned.1.call-done = bf16[240,1,768]{2,0,1:T(8,128)(2,1)} async-done(((bf16[960,1,768]{2,0,1:T(8,128)(2,1)}), bf16[240,1,768]{2,0,1:T(8,128)(2,1)}) %reduce-scatter.47.cloned.1.call-update) | async-done | bytes 368656 | tf_op jit(solution)/shard_map/reduce_scatter | solution.py:309
  1247.3 34.9 %reduce-scatter.43.cloned.1.call-done = bf16[240,1,768]{2,0,1:T(8,128)(2,1)} async-done(((bf16[960,1,768]{2,0,1:T(8,128)(2,1)}), bf16[240,1,768]{2,0,1:T(8,128)(2,1)}) %reduce-scatter.43.cloned.1.call-update) | async-done | bytes 368656 | tf_op jit(solution)/shard_map/reduce_scatter | solution.py:309
  1282.2 35.6 %reduce-scatter.39.cloned.1.call-done = bf16[240,1,768]{2,0,1:T(8,128)(2,1)} async-done(((bf16[960,1,768]{2,0,1:T(8,128)(2,1)}), bf16[240,1,768]{2,0,1:T(8,128)(2,1)}) %reduce-scatter.39.cloned.1.call-update) | async-done | bytes 368656 | tf_op jit(solution)/shard_map/reduce_scatter | solution.py:309
  1326.8 40.3 %all-reduce = (f32[768]{0:T(1024)}, f32[768]{0:T(1024)}, f32[768]{0:T(1024)}, f32[768]{0:T(1024)}, f32[768]{0:T(1024)}, /*index=5*/f32[768]{0:T(1024)}, f32[5,768]{1,0:T(8,128)}) all-reduce(f32[768]{0:T(1024)S(1)} %add_add_fusion.33, f32[768]{0:T(1024)S(1)} %add_add_fusion.31, ...), channel_id=1, replica_groups=mesh['batch'=8,'tensor'=4] {'batch','tensor'}, use_global_device_ids=true, to_apply=%region_82.85 | all-reduce | flops 8448 | bytes 67584 | tf_op jit(solution)/shard_map/psum | solution.py:365
  (656 shorter events, 337.0 us)
Async XLA Ops:
  7.2 385.5 %copy-start = (bf16[768,768]{1,0:T(8,128)(2,1)S(1)}, bf16[768,768]{1,0:T(8,128)(2,1)}, u32[]{:S(2)}) copy-start(bf16[768,768]{1,0:T(8,128)(2,1)} %param.30) | copy-start | bytes 3538948
  7.2 59.7 %all-gather.15.cloned.1.call-start = ((), (), s32[]{:S(2)}) async-start(), calls=%async_computation.20 | async-start | bytes 1843200 | tf_op jit(solution)/shard_map/all_gather | solution.py:273
  28.7 74.7 %all-gather.19.cloned.1.call-start = ((), (), s32[]{:S(2)}) async-start(), calls=%async_computation.24 | async-start | bytes 1843200 | tf_op jit(solution)/shard_map/all_gather | solution.py:273
  29.4 110.4 %all-gather.23.cloned.1.call-start = ((), (), s32[]{:S(2)}) async-start(), calls=%async_computation.28 | async-start | bytes 1843200 | tf_op jit(solution)/shard_map/all_gather | solution.py:273
  30.2 145.4 %all-gather.27.cloned.1.call-start = ((), (), s32[]{:S(2)}) async-start(), calls=%async_computation.32 | async-start | bytes 1843200 | tf_op jit(solution)/shard_map/all_gather | solution.py:273
  30.8 180.5 %reduce-scatter.21.cloned.1.call-start = ((), (), s32[]{:S(2)}) async-start(), calls=%async_computation.21 | async-start | bytes 1843200 | tf_op jit(solution)/shard_map/reduce_scatter | solution.py:276
  33.7 144.4 %copy-start.82 = (f32[3,64]{1,0:T(4,128)}, f32[3,64]{1,0:T(4,128)S(1)}, u32[]{:S(2)}) copy-start(f32[3,64]{1,0:T(4,128)S(1)} %reshape.2254) | copy-start | bytes 2308
  81.5 165.2 %reduce-scatter.25.cloned.1.call-start = ((), (), s32[]{:S(2)}) async-start(), calls=%async_computation.25 | async-start | bytes 1843200 | tf_op jit(solution)/shard_map/reduce_scatter | solution.py:276
  118.0 164.3 %reduce-scatter.29.cloned.1.call-start = ((), (), s32[]{:S(2)}) async-start(), calls=%async_computation.29 | async-start | bytes 1843200 | tf_op jit(solution)/shard_map/reduce_scatter | solution.py:276
  154.2 163.1 %reduce-scatter.33.cloned.1.call-start = ((), (), s32[]{:S(2)}) async-start(), calls=%async_computation.33 | async-start | bytes 1843200 | tf_op jit(solution)/shard_map/reduce_scatter | solution.py:276
  189.7 167.2 %all-gather.29.cloned.1.call-start = ((), (), s32[]{:S(2)}) async-start(), calls=%async_computation.34 | async-start | bytes 1843200 | tf_op jit(solution)/shard_map/all_gather | solution.py:284
  322.6 70.0 %all-gather.37.cloned.1.call-start = ((), (), s32[]{:S(2)}) async-start(), calls=%async_computation.45 | async-start | bytes 1843200 | tf_op jit(solution)/shard_map/all_gather | solution.py:295
  332.6 96.6 %all-gather.25.cloned.1.call-start = ((), (), s32[]{:S(2)}) async-start(), calls=%async_computation.30 | async-start | bytes 1843200 | tf_op jit(solution)/shard_map/all_gather | solution.py:284
  333.3 131.6 %all-gather.35.cloned.1.call-start = ((), (), s32[]{:S(2)}) async-start(), calls=%async_computation.42 | async-start | bytes 1843200 | tf_op jit(solution)/shard_map/all_gather | solution.py:295
  336.6 164.1 %all-gather.21.cloned.1.call-start = ((), (), s32[]{:S(2)}) async-start(), calls=%async_computation.26 | async-start | bytes 1843200 | tf_op jit(solution)/shard_map/all_gather | solution.py:284
  337.4 199.1 %all-gather.33.cloned.1.call-start = ((), (), s32[]{:S(2)}) async-start(), calls=%async_computation.39 | async-start | bytes 1843200 | tf_op jit(solution)/shard_map/all_gather | solution.py:295
  340.7 232.1 %all-gather.17.cloned.1.call-start = ((), (), s32[]{:S(2)}) async-start(), calls=%async_computation.22 | async-start | bytes 1843200 | tf_op jit(solution)/shard_map/all_gather | solution.py:284
  341.3 267.2 %all-gather.31.cloned.1.call-start = ((), (), s32[]{:S(2)}) async-start(), calls=%async_computation.36 | async-start | bytes 1843200 | tf_op jit(solution)/shard_map/all_gather | solution.py:295
  344.7 312.2 %reduce-scatter.49.cloned.1.call-start = ((), (), s32[]{:S(2)}) async-start(), calls=%async_computation.46 | async-start | bytes 1843200 | tf_op jit(solution)/shard_map/reduce_scatter | solution.py:298
  402.3 276.8 %reduce-scatter.45.cloned.1.call-start = ((), (), s32[]{:S(2)}) async-start(), calls=%async_computation.43 | async-start | bytes 1843200 | tf_op jit(solution)/shard_map/reduce_scatter | solution.py:298
  474.5 240.2 %reduce-scatter.31.cloned.1.call-start = ((), (), s32[]{:S(2)}) async-start(), calls=%async_computation.31 | async-start | bytes 1843200 | tf_op jit(solution)/shard_map/reduce_scatter | solution.py:287
  479.5 270.1 %reduce-scatter.41.cloned.1.call-start = ((), (), s32[]{:S(2)}) async-start(), calls=%async_computation.40 | async-start | bytes 1843200 | tf_op jit(solution)/shard_map/reduce_scatter | solution.py:298
  546.1 239.1 %reduce-scatter.37.cloned.1.call-start = ((), (), s32[]{:S(2)}) async-start(), calls=%async_computation.37 | async-start | bytes 1843200 | tf_op jit(solution)/shard_map/reduce_scatter | solution.py:298
  618.2 214.6 %reduce-scatter.35.cloned.1.call-start = ((), (), s32[]{:S(2)}) async-start(), calls=%async_computation.35 | async-start | bytes 1843200 | tf_op jit(solution)/shard_map/reduce_scatter | solution.py:287
  623.2 257.8 %reduce-scatter.23.cloned.1.call-start = ((), (), s32[]{:S(2)}) async-start(), calls=%async_computation.23 | async-start | bytes 1843200 | tf_op jit(solution)/shard_map/reduce_scatter | solution.py:287
  628.2 293.8 %reduce-scatter.27.cloned.1.call-start = ((), (), s32[]{:S(2)}) async-start(), calls=%async_computation.27 | async-start | bytes 1843200 | tf_op jit(solution)/shard_map/reduce_scatter | solution.py:287
  633.7 375.4 %reduce-scatter.57.cloned.1.call-start = ((), (), s32[]{:S(2)}) async-start(), calls=%async_computation.52 | async-start | bytes 2654208 | tf_op jit(solution)/shard_map/reduce_scatter | solution.py:343
  644.0 368.5 %reduce-scatter.59.cloned.1.call-start = ((), (), s32[]{:S(2)}) async-start(), calls=%async_computation.53 | async-start | bytes 2654208 | tf_op jit(solution)/shard_map/reduce_scatter | solution.py:344
  656.8 510.4 %reduce-scatter.55.cloned.1.call-start = ((), (), s32[]{:S(2)}) async-start(), calls=%async_computation.51 | async-start | bytes 663552 | tf_op jit(solution)/shard_map/reduce_scatter | solution.py:342
  789.9 137.3 %collective-permute-start.8 = (bf16[240,1,768]{2,0,1:T(8,128)(2,1)}, bf16[240,1,768]{2,0,1:T(8,128)(2,1)}, u32[]{:S(2)}, u32[]{:S(2)}) collective-permute-start(bf16[240,1,768]{2,0,1:T(8,128)(2,1)} %convert_element_type.831), channel_id=1, source_target_pairs={{0,3},{1,0},{2,1},{3,2},{4,7},{5,4},{6,5},{7,6},{8,11},{9,8},{10,9... | collective-permute-start | bytes 1105928 | tf_op jit(solution)/shard_map/ppermute | solution.py:25
  791.1 92.8 %collective-permute-start.6 = (bf16[240,1,768]{2,0,1:T(8,128)(2,1)}, bf16[240,1,768]{2,0,1:T(8,128)(2,1)}, u32[]{:S(2)}, u32[]{:S(2)}) collective-permute-start(bf16[240,1,768]{2,0,1:T(8,128)(2,1)} %convert_element_type.831), channel_id=1, source_target_pairs={{0,1},{1,2},{2,3},{3,0},{4,5},{5,6},{6,7},{7,4},{8,9},{9,10},{10,1... | collective-permute-start | bytes 1105928 | tf_op jit(solution)/shard_map/ppermute | solution.py:23
  836.6 99.2 %collective-permute-start.11 = (bf16[240,1,768]{2,0,1:T(8,128)(2,1)}, bf16[240,1,768]{2,0,1:T(8,128)(2,1)}, u32[]{:S(2)}, u32[]{:S(2)}) collective-permute-start(bf16[240,1,768]{2,0,1:T(8,128)(2,1)} %convert_element_type.847), channel_id=1, source_target_pairs={{0,3},{1,0},{2,1},{3,2},{4,7},{5,4},{6,5},{7,6},{8,11},{9,8},{10,9... | collective-permute-start | bytes 1105928 | tf_op jit(solution)/shard_map/ppermute | solution.py:25
  839.9 87.5 %collective-permute-start.9 = (bf16[240,1,768]{2,0,1:T(8,128)(2,1)}, bf16[240,1,768]{2,0,1:T(8,128)(2,1)}, u32[]{:S(2)}, u32[]{:S(2)}) collective-permute-start(bf16[240,1,768]{2,0,1:T(8,128)(2,1)} %convert_element_type.847), channel_id=1, source_target_pairs={{0,1},{1,2},{2,3},{3,0},{4,5},{5,6},{6,7},{7,4},{8,9},{9,10},{10,1... | collective-permute-start | bytes 1105928 | tf_op jit(solution)/shard_map/ppermute | solution.py:23
  883.9 44.1 %collective-permute-start.7 = (bf16[240,1,768]{2,0,1:T(8,128)(2,1)}, bf16[240,1,768]{2,0,1:T(8,128)(2,1)S(1)}, u32[]{:S(2)}, u32[]{:S(2)}) collective-permute-start(bf16[240,1,768]{2,0,1:T(8,128)(2,1)} %collective-permute-done.6), channel_id=1, source_target_pairs={{0,1},{1,2},{2,3},{3,0},{4,5},{5,6},{6,7},{7,4},{8,9},{9,10},{10,1... | collective-permute-start | bytes 1105928 | tf_op jit(solution)/shard_map/ppermute | solution.py:23
  925.4 69.9 %collective-permute-start.2 = (bf16[240,1,768]{2,0,1:T(8,128)(2,1)S(1)}, bf16[240,1,768]{2,0,1:T(8,128)(2,1)S(1)}, u32[]{:S(2)}, u32[]{:S(2)}) collective-permute-start(bf16[240,1,768]{2,0,1:T(8,128)(2,1)S(1)} %convert_element_type.799), channel_id=1, source_target_pairs={{0,3},{1,0},{2,1},{3,2},{4,7},{5,4},{6,5},{7,6},{8,11},{9,8},{10,9... | collective-permute-start | bytes 1105928 | tf_op jit(solution)/shard_map/ppermute | solution.py:25
  927.2 17.8 %collective-permute-start = (bf16[240,1,768]{2,0,1:T(8,128)(2,1)S(1)}, bf16[240,1,768]{2,0,1:T(8,128)(2,1)S(1)}, u32[]{:S(2)}, u32[]{:S(2)}) collective-permute-start(bf16[240,1,768]{2,0,1:T(8,128)(2,1)S(1)} %convert_element_type.799), channel_id=1, source_target_pairs={{0,1},{1,2},{2,3},{3,0},{4,5},{5,6},{6,7},{7,4},{8,9},{9,10},{10,1... | collective-permute-start | bytes 1105928 | tf_op jit(solution)/shard_map/ppermute | solution.py:23
  927.5 25.4 %collective-permute-start.3 = (bf16[240,1,768]{2,0,1:T(8,128)(2,1)S(1)}, bf16[240,1,768]{2,0,1:T(8,128)(2,1)S(1)}, u32[]{:S(2)}, u32[]{:S(2)}) collective-permute-start(bf16[240,1,768]{2,0,1:T(8,128)(2,1)S(1)} %convert_element_type.815), channel_id=1, source_target_pairs={{0,1},{1,2},{2,3},{3,0},{4,5},{5,6},{6,7},{7,4},{8,9},{9,10},{10,1... | collective-permute-start | bytes 1105928 | tf_op jit(solution)/shard_map/ppermute | solution.py:23
  928.8 31.9 %collective-permute-start.10 = (bf16[240,1,768]{2,0,1:T(8,128)(2,1)}, bf16[240,1,768]{2,0,1:T(8,128)(2,1)S(1)}, u32[]{:S(2)}, u32[]{:S(2)}) collective-permute-start(bf16[240,1,768]{2,0,1:T(8,128)(2,1)} %collective-permute-done.9), channel_id=1, source_target_pairs={{0,1},{1,2},{2,3},{3,0},{4,5},{5,6},{6,7},{7,4},{8,9},{9,10},{10,1... | collective-permute-start | bytes 1105928 | tf_op jit(solution)/shard_map/ppermute | solution.py:23
  935.8 32.7 %collective-permute-start.5 = (bf16[240,1,768]{2,0,1:T(8,128)(2,1)S(1)}, bf16[240,1,768]{2,0,1:T(8,128)(2,1)S(1)}, u32[]{:S(2)}, u32[]{:S(2)}) collective-permute-start(bf16[240,1,768]{2,0,1:T(8,128)(2,1)S(1)} %convert_element_type.815), channel_id=1, source_target_pairs={{0,3},{1,0},{2,1},{3,2},{4,7},{5,4},{6,5},{7,6},{8,11},{9,8},{10,9... | collective-permute-start | bytes 1105928 | tf_op jit(solution)/shard_map/ppermute | solution.py:25
  944.9 50.3 %collective-permute-start.1 = (bf16[240,1,768]{2,0,1:T(8,128)(2,1)S(1)}, bf16[240,1,768]{2,0,1:T(8,128)(2,1)S(1)}, u32[]{:S(2)}, u32[]{:S(2)}) collective-permute-start(bf16[240,1,768]{2,0,1:T(8,128)(2,1)S(1)} %collective-permute-done), channel_id=1, source_target_pairs={{0,1},{1,2},{2,3},{3,0},{4,5},{5,6},{6,7},{7,4},{8,9},{9,10},{10,1... | collective-permute-start | bytes 1105928 | tf_op jit(solution)/shard_map/ppermute | solution.py:23
  952.8 30.6 %collective-permute-start.4 = (bf16[240,1,768]{2,0,1:T(8,128)(2,1)S(1)}, bf16[240,1,768]{2,0,1:T(8,128)(2,1)S(1)}, u32[]{:S(2)}, u32[]{:S(2)}) collective-permute-start(bf16[240,1,768]{2,0,1:T(8,128)(2,1)S(1)} %collective-permute-done.3), channel_id=1, source_target_pairs={{0,1},{1,2},{2,3},{3,0},{4,5},{5,6},{6,7},{7,4},{8,9},{9,10},{10,1... | collective-permute-start | bytes 1105928 | tf_op jit(solution)/shard_map/ppermute | solution.py:23
  1008.9 169.8 %all-gather.39.cloned.1.call-start = ((), (), s32[]{:S(2)}) async-start(), calls=%async_computation.48 | async-start | bytes 1327104 | tf_op jit(solution)/shard_map/all_gather | solution.py:358
  1010.7 170.9 %all-gather.41.cloned.1.call-start = ((), (), s32[]{:S(2)}) async-start(), calls=%async_computation.49 | async-start | bytes 1327104 | tf_op jit(solution)/shard_map/all_gather | solution.py:361
  1014.1 170.5 %reduce-scatter.53.cloned.1.call-start = ((), (), s32[]{:S(2)}) async-start(), calls=%async_computation.50 | async-start | bytes 2654208 | tf_op jit(solution)/shard_map/reduce_scatter | solution.py:341
  1132.5 79.7 %reduce-scatter.51.cloned.1.call-start = ((), (), s32[]{:S(2)}) async-start(), calls=%async_computation.47 | async-start | bytes 1843200 | tf_op jit(solution)/shard_map/reduce_scatter | solution.py:309
  1136.3 111.0 %reduce-scatter.47.cloned.1.call-start = ((), (), s32[]{:S(2)}) async-start(), calls=%async_computation.44 | async-start | bytes 1843200 | tf_op jit(solution)/shard_map/reduce_scatter | solution.py:309
  1140.5 141.7 %reduce-scatter.43.cloned.1.call-start = ((), (), s32[]{:S(2)}) async-start(), calls=%async_computation.41 | async-start | bytes 1843200 | tf_op jit(solution)/shard_map/reduce_scatter | solution.py:309
  1144.4 173.4 %reduce-scatter.39.cloned.1.call-start = ((), (), s32[]{:S(2)}) async-start(), calls=%async_computation.38 | async-start | bytes 1843200 | tf_op jit(solution)/shard_map/reduce_scatter | solution.py:309
  (175 other events, 3126.9 us)
Sparse Core Ops, SparseCore 0:
  28.8 38.0 all-gather.14
  69.0 34.3 all-gather.18
  105.5 34.2 all-gather.22
  141.3 34.2 all-gather.26
  178.3 32.8 reduce-scatter.20
  214.0 32.6 reduce-scatter.24
  249.6 32.6 reduce-scatter.28
  284.6 32.6 reduce-scatter.32
  322.8 34.1 all-gather.28
  358.4 34.2 all-gather.36
  394.8 34.2 all-gather.24
  430.6 34.2 all-gather.34
  466.4 34.2 all-gather.20
  502.2 34.2 all-gather.32
  538.5 34.2 all-gather.16
  574.2 34.2 all-gather.30
  610.7 32.8 reduce-scatter.48
  646.4 32.6 reduce-scatter.44
  682.0 32.6 reduce-scatter.30
  716.9 32.6 reduce-scatter.40
  752.5 32.6 reduce-scatter.36
  787.5 45.1 reduce-scatter.34
  835.1 45.8 reduce-scatter.22
  883.2 38.7 reduce-scatter.26
  925.3 41.4 reduce-scatter.56
  970.1 42.3 reduce-scatter.58
  1016.0 34.3 reduce-scatter.54
  1052.2 23.9 all-gather.38
  1078.1 23.9 all-gather.40
  1132.7 43.3 reduce-scatter.52
  1178.4 33.8 reduce-scatter.50
  1214.6 32.6 reduce-scatter.46
  1249.5 32.6 reduce-scatter.42
  1285.1 32.6 reduce-scatter.38
